TPU v7x, 256 devices: a whole 4x4x8 slice. The times are simulated.
256 devices in a mesh: box: 16 (over x_lo, y, core), samp: 16 (over z, x_hi).
Axes of the slice: x: 4 (x_hi: 2, x_lo: 2; x = x_hi * 2 + x_lo), y: 4, z: 8, core: 2. Of those that a mesh axis runs over, the one named last changes fastest.
Arguments:
- xvec: bfloat16 [4096, 2, 4, 128], P(('box', 'samp')), may hold values from -6 to 6
- near_blocks: bfloat16 [4096, 8, 2, 128, 128], P(('box', 'samp')), may hold values from -0.1875 to 0.1875
- neighbours: int32 [4096, 8], P(('box', 'samp')), may hold values from 0 to 4095, as said below
- lift: bfloat16 [4096, 2, 128, 128], P(('box', 'samp')), may hold values from -0.5 to 0.5
- place: bfloat16 [4096, 2, 128, 128], P(('box', 'samp')), may hold values from -0.25 to 0.25
- interp: bfloat16 [2048, 128], replicated, may hold values from -0.5 to 0.5
- phases: float32 [8, 2, 2048], replicated, may hold values from -1 to 1, as said below
- octant: int32 [4096], P(('box', 'samp')), may hold values from 0 to 7, as said below
- leaf_parent_index: int32 [4096], P(('box', 'samp')), may hold values from 0 to 511, as said below
- translators: float32 [64, 2, 2048], P(None, None, 'samp'), may hold values from -0.5 to 0.5
- inter_list: int32 [512, 16], P('box'), may hold values from 0 to 511, as said below
- trans_id: int32 [512, 16], P('box'), may hold values from 0 to 63
Outputs:
- product: float32 [4096, 2, 4, 128], P(('box', 'samp'))
Inputs may be any that keep to these rules, and one draw needn't show every extreme that they name: `neighbours`: row n starts with n itself; its other entries are distinct and lie within 8 boxes of n in cyclic order over all 4096 leaf boxes (the texture is periodic). `leaf_parent_index`: leaf box n belongs to box group g = n // 256 and its parent is one of that group's upper-level boxes g * 32 to g * 32 + 31; every upper-level box has exactly 8 children. `octant`: the 8 children of an upper-level box have 8 distinct octants. `inter_list`: entries of row p are distinct, each equal to p + d modulo 512 with 2 <= |d| <= 32 (the periodic tree's interaction zone). `phases`: each entry has magnitude one: real part squared plus imaginary part squared is 1.
All inputs are finite; a program needn't handle non-finite values.
Results may differ from a plain program's by a relative error of at most 0.0065.
Values may be sent and summed in bfloat16 or wider, within the bound.
A program may use at most 64 MiB of HBM per device.

v0:
```python
import jax
import jax.numpy as jnp
from jax import lax
from jax.sharding import PartitionSpec as P


def with_halo(cells, sides, width):
    for axis, dim in sides:
        count = lax.axis_size(axis)
        head = lax.slice_in_dim(cells, 0, width, axis=dim)
        tail = lax.slice_in_dim(cells, cells.shape[dim] - width, cells.shape[dim], axis=dim)
        cells = jnp.concatenate(
            [
                lax.ppermute(tail, axis, [(i, (i + 1) % count) for i in range(count)]),
                cells,
                lax.ppermute(head, axis, [((i + 1) % count, i) for i in range(count)]),
            ],
            axis=dim,
        )
    return cells


def cmul(ar, ai, br, bi):
    return (ar * br - ai * bi, ar * bi + ai * br)


def on_device(
    xvec,
    near_blocks,
    neighbours,
    lift,
    place,
    interp,
    phases,
    octant,
    leaf_parent_index,
    translators,
    inter_list,
    trans_id,
):
    f32 = jnp.float32
    bf16 = jnp.bfloat16
    finest_precision = lax.Precision.HIGHEST
    boxes = xvec.shape[0]
    nsamp = lax.axis_size("samp")
    nboxaxis = lax.axis_size("box")
    box_index = lax.axis_index("box")
    samp_index = lax.axis_index("samp")
    compute_unit = box_index * nsamp + samp_index
    total = boxes * nsamp * nboxaxis
    reach = boxes // 2
    parents_here = boxes * nsamp // 8
    all_parents = parents_here * nboxaxis
    sample_share = interp.shape[0] // nsamp
    rhs_count = xvec.shape[2]
    widened = with_halo(xvec, ((("box", "samp"), 0),), reach)
    local_index = jnp.mod(neighbours - compute_unit * boxes + reach, total)
    near_x = jnp.take(widened, local_index, axis=0)

    def apply(a, b):
        return jnp.einsum("bkpq,bkrq->brp", a, b, preferred_element_type=f32)

    near_r = apply(near_blocks[:, :, 0], near_x[:, :, 0]) - apply(
        near_blocks[:, :, 1], near_x[:, :, 1]
    )
    near_i = apply(near_blocks[:, :, 0], near_x[:, :, 1]) + apply(
        near_blocks[:, :, 1], near_x[:, :, 0]
    )

    def radiate(a, b):
        return jnp.einsum("bqu,bru->brq", a, b, preferred_element_type=f32)

    pat_r = radiate(lift[:, 0], xvec[:, 0]) - radiate(lift[:, 1], xvec[:, 1])
    pat_i = radiate(lift[:, 0], xvec[:, 1]) + radiate(lift[:, 1], xvec[:, 0])
    pattern = jnp.stack([pat_r, pat_i], 1).astype(bf16)

    def phase_rows(octs):
        indicator_matrix = (octs[:, None] == jnp.arange(8, dtype=jnp.int32)[None, :]).astype(f32)
        return jnp.einsum("ex,xwf->ewf", indicator_matrix, phases, precision=finest_precision)

    def parent_table(pars):
        local = pars - box_index * parents_here
        return local[:, None] == jnp.arange(parents_here, dtype=jnp.int32)[None, :]

    rows_i = interp
    raised_terms = jnp.einsum("sq,bcrq->bcrs", rows_i, pattern, preferred_element_type=f32)
    shift = phase_rows(octant)
    cr, ci = cmul(
        shift[:, 0][:, None, :], shift[:, 1][:, None, :], raised_terms[:, 0], raised_terms[:, 1]
    )
    owner = parent_table(leaf_parent_index).astype(f32)
    sum_r = jnp.einsum("bp,brs->prs", owner, cr, precision=finest_precision)
    sum_i = jnp.einsum("bp,brs->prs", owner, ci, precision=finest_precision)
    term = jnp.stack([sum_r, sum_i], 1)
    term = term.reshape(parents_here, 2, rhs_count, 1 * lax.axis_size("samp"), sample_share)
    upward = lax.psum_scatter(
        jnp.transpose(term, (3, 0, 1, 2, 4)), "samp", scatter_dimension=0, tiled=True
    )[0]
    parent_pat = upward.astype(bf16)
    table_count = translators.shape[0]
    selector_index = (
        trans_id[:, :, None] == jnp.arange(table_count, dtype=jnp.int32)[None, None, :]
    ).astype(f32)
    operator_list = jnp.einsum(
        "yaw,wjt->yajt", selector_index, translators, precision=finest_precision
    )
    bordered = with_halo(parent_pat, (("box", 0),), parents_here)
    window_index = jnp.mod(inter_list - box_index * parents_here + parents_here, all_parents)
    select = (
        window_index[:, :, None] == jnp.arange(3 * parents_here, dtype=jnp.int32)[None, None, :]
    ).astype(bf16)
    fetched = jnp.einsum("pkj,jcrs->pkcrs", select, bordered, preferred_element_type=f32)
    tr_r = operator_list[:, :, 0][:, :, None, :]
    tr_i = operator_list[:, :, 1][:, :, None, :]
    add_r, add_i = cmul(tr_r, tr_i, fetched[:, :, 0], fetched[:, :, 1])
    incoming = jnp.stack([add_r.sum(1), add_i.sum(1)], 1).astype(bf16)
    owner = parent_table(leaf_parent_index).astype(bf16)
    chosen = jnp.einsum(
        "ei,ihfz->ehfz",
        owner,
        lax.all_gather(incoming, "samp", axis=3, tiled=True),
        preferred_element_type=f32,
    )
    shift = phase_rows(octant)
    sr, si = cmul(shift[:, 0][:, None, :], shift[:, 1][:, None, :], chosen[:, 0], chosen[:, 1])
    shifted = jnp.stack([sr, si], 1).astype(bf16)
    rows_i = interp
    field = jnp.einsum("bcrs,sq->bcrq", shifted, rows_i, preferred_element_type=f32)
    field = field.astype(bf16)

    def receive(a, b):
        return jnp.einsum("buq,brq->bru", a, b, preferred_element_type=f32)

    far_r = receive(place[:, 0], field[:, 0]) - receive(place[:, 1], field[:, 1])
    far_i = receive(place[:, 0], field[:, 1]) + receive(place[:, 1], field[:, 0])
    return jnp.stack([near_r + far_r, near_i + far_i], 1)


def solution(mesh):
    in_specs = (
        P(("box", "samp"), None, None, None),
        P(("box", "samp"), None, None, None, None),
        P(("box", "samp"), None),
        P(("box", "samp"), None, None, None),
        P(("box", "samp"), None, None, None),
        P(),
        P(),
        P(("box", "samp")),
        P(("box", "samp")),
        P(None, None, "samp"),
        P("box", None),
        P("box", None),
    )
    out_specs = P(("box", "samp"), None, None, None)
    return jax.shard_map(
        on_device, mesh=mesh, in_specs=in_specs, out_specs=out_specs, check_vma=False
    )
```

profile of v0, /device:TPU:8, one launch (start us, length us, event | category | flops | bytes accessed | tf_op | source)
XLA Modules:
  0.0 224.2 jit_solution(11524168463856257246)
XLA Ops:
  6.5 1.5 fusion.53
  8.0 1.4 fusion.55
  9.5 1.3 fusion.79
  10.8 1.4 fusion.36
  12.2 1.4 fusion.37
  14.2 0.7 convolution_bitcast_fusion
  14.9 0.7 convolution_bitcast_fusion.1
  15.8 115.4 %all-reduce.2 = bf16[16,32,2,4,128]{4,1,0,3,2:T(8,128)(2,1)} all-reduce(f32[16,32,2,4,128]{4,1,0,3,2:T(8,128)S(1)} %maximum_bitcast_fusion), channel_id=2, replica_groups=mesh['box'=16,'samp'=16] {'samp'}, use_global_device_ids=true, to_apply=%region_0.1.clone | all-reduce | flops 524288 | bytes 3145728
  131.2 0.6 dynamic-slice
  131.8 1.5 fusion.83
  133.3 1.7 collective-permute-start.3
  135.1 2.6 %collective-permute-start = (bf16[8,2,4,128]{3,2,1,0:T(4,128)(2,1)S(1)}, bf16[8,2,4,128]{3,2,1,0:T(4,128)(2,1)S(1)}, u32[]{:S(2)}, u32[]{:S(2)}) collective-permute-start(bf16[8,2,4,128]{3,2,1,0:T(4,128)(2,1)S(1)} %get-tuple-element.19), channel_id=1, source_target_pairs={{0,1},{1,2},{2,3},{3,4},{4,5},{5,6},{6,7},{7,8},{8,9},{9,10},{10,1... | collective-permute-start | bytes 49160 | tf_op jit(solution)/shard_map/ppermute | solution.py:14
  137.7 3.7 %collective-permute-start.1 = (bf16[8,2,4,128]{3,2,1,0:T(4,128)(2,1)S(1)}, bf16[8,2,4,128]{3,2,1,0:T(4,128)(2,1)S(1)}, u32[]{:S(2)}, u32[]{:S(2)}) collective-permute-start(bf16[8,2,4,128]{3,2,1,0:T(4,128)(2,1)S(1)} %get-tuple-element.20), channel_id=1, source_target_pairs={{1,0},{2,1},{3,2},{4,3},{5,4},{6,5},{7,6},{8,7},{9,8},{10,9},{11,1... | collective-permute-start | bytes 49160 | tf_op jit(solution)/shard_map/ppermute | solution.py:16
  142.1 0.5 fusion.72
  142.6 0.7 subtract_reduce_fusion
  143.3 0.6 pad_maximum_fusion.1
  144.3 0.8 gather_fusion
  145.4 3.4 %fusion.12 = f32[16,4,128]{2,1,0:T(4,128)S(1)} fusion(bf16[16,8,2,128,128]{4,3,2,1,0:T(8,128)(2,1)} %param.13, bf16[16,8,2,4,128]{4,3,1,0,2:T(4,128)(2,1)S(1)} %broadcast_select_fusion), kind=kOutput, calls=%fused_computation.17 | convolution fusion | flops 16777216 | bytes 4358144 | tf_op jit(solution)/shard_map/bkpq,bkrq->brp/dot_general | solution.py:61
  148.8 3.5 %fusion.15 = f32[16,4,128]{2,1,0:T(4,128)S(1)} fusion(bf16[16,8,2,128,128]{4,3,2,1,0:T(8,128)(2,1)} %param.13, bf16[16,8,2,4,128]{4,3,1,0,2:T(4,128)(2,1)S(1)} %broadcast_select_fusion), kind=kOutput, calls=%fused_computation.18 | convolution fusion | flops 16777216 | bytes 4358144 | tf_op jit(solution)/shard_map/bkpq,bkrq->brp/dot_general | solution.py:61
  152.3 3.4 %fusion.31 = f32[16,4,128]{2,1,0:T(4,128)S(1)} fusion(f32[16,4,128]{2,1,0:T(4,128)S(1)} %fusion.12, bf16[16,8,2,128,128]{4,3,2,1,0:T(8,128)(2,1)} %param.13, bf16[16,8,2,4,128]{4,3,1,0,2:T(4,128)(2,1)S(1)} %broadcast_select_fusion), kind=kOutput, calls=%fused_computation.30 | convolution fusion | flops 16785408 | bytes 4390912 | tf_op jit(solution)/shard_map/bkpq,bkrq->brp/dot_general | solution.py:61
  155.7 3.5 %fusion.28 = f32[16,4,128]{2,1,0:T(4,128)S(1)} fusion(f32[16,4,128]{2,1,0:T(4,128)S(1)} %fusion.15, bf16[16,8,2,128,128]{4,3,2,1,0:T(8,128)(2,1)} %param.13, bf16[16,8,2,4,128]{4,3,1,0,2:T(4,128)(2,1)S(1)} %broadcast_select_fusion), kind=kOutput, calls=%fused_computation.29 | convolution fusion | flops 16785408 | bytes 4390912 | tf_op jit(solution)/shard_map/bkpq,bkrq->brp/dot_general | solution.py:61
  159.2 53.9 %all-gather.2.cloned.1.call-done = bf16[32,2,4,2048]{3,0,2,1:T(8,128)(2,1)} async-done(((bf16[32,2,4,128]{3,0,2,1:T(8,128)(2,1)}), bf16[32,2,4,2048]{3,0,2,1:T(8,128)(2,1)}) %all-gather.2.cloned.1.call-update) | async-done | bytes 1048592 | tf_op jit(solution)/shard_map/all_gather | solution.py:121
  213.1 1.6 fusion.103
  216.7 0.6 copy.87
  (54 shorter events, 4.0 us)
Async XLA Ops:
  6.5 7.2 %copy-start = (bf16[2048,128]{1,0:T(8,128)(2,1)S(1)}, bf16[2048,128]{1,0:T(8,128)(2,1)}, u32[]{:S(2)}) copy-start(bf16[2048,128]{1,0:T(8,128)(2,1)} %param.17) | copy-start | bytes 1572868
  6.5 7.5 %copy-start.7 = (s32[16]{0:T(128)S(1)}, s32[16]{0:T(128)}, u32[]{:S(2)}) copy-start(s32[16]{0:T(128)} %param.20) | copy-start | bytes 196
  6.5 206.5 %all-gather.2.cloned.1.call-start = ((), (), s32[]{:S(2)}) async-start(), calls=%async_computation | async-start | bytes 1114112 | tf_op jit(solution)/shard_map/all_gather | solution.py:121
  14.9 116.4 %copy-start.8 = (u32[256]{0:T(256)S(1)}, u32[256]{0:T(256)}, u32[]{:S(2)}) copy-start(u32[256]{0:T(256)} %constant.68) | copy-start | bytes 3076
  14.9 120.2 %copy-start.2 = (bf16[16,2,4,128]{3,2,1,0:T(4,128)(2,1)S(1)}, bf16[16,2,4,128]{3,2,1,0:T(4,128)(2,1)}, u32[]{:S(2)}) copy-start(bf16[16,2,4,128]{3,2,1,0:T(4,128)(2,1)} %param.12) | copy-start | bytes 98308
  14.9 126.5 %copy-start.4 = (s32[32,16]{0,1:T(8,128)S(1)}, s32[32,16]{0,1:T(8,128)}, u32[]{:S(2)}) copy-start(s32[32,16]{0,1:T(8,128)} %param.23) | copy-start | bytes 6148
  14.9 126.6 %copy-start.3 = (f32[64,2,128]{2,1,0:T(2,128)S(1)}, f32[64,2,128]{2,1,0:T(2,128)}, u32[]{:S(2)}) copy-start(f32[64,2,128]{2,1,0:T(2,128)} %param.21) | copy-start | bytes 196612
  15.6 126.4 %copy-start.5 = (s32[32,16]{0,1:T(8,128)S(1)}, s32[32,16]{0,1:T(8,128)}, u32[]{:S(2)}) copy-start(s32[32,16]{0,1:T(8,128)} %param.22) | copy-start | bytes 6148
  131.2 12.7 %copy-start.6 = (s32[16,8]{0,1:T(8,128)S(1)}, s32[16,8]{0,1:T(8,128)}, u32[]{:S(2)}) copy-start(s32[16,8]{0,1:T(8,128)} %param.14) | copy-start | bytes 1540
  133.3 8.8 %collective-permute-start.2 = (bf16[32,2,4,128]{3,0,2,1:T(8,128)(2,1)S(1)}, bf16[32,2,4,128]{3,0,2,1:T(8,128)(2,1)S(1)}, u32[]{:S(2)}, u32[]{:S(2)}) collective-permute-start(bf16[32,2,4,128]{3,0,2,1:T(8,128)(2,1)S(1)} %fusion.83), channel_id=1, source_target_pairs={{0,16},{16,32},{32,48},{48,64},{64,80},{80,96},{96,112},{112,128},... | collective-permute-start | bytes 196616 | tf_op jit(solution)/shard_map/ppermute | solution.py:14
  133.3 8.8 %collective-permute-start.3 = (bf16[32,2,4,128]{3,0,2,1:T(8,128)(2,1)S(1)}, bf16[32,2,4,128]{3,0,2,1:T(8,128)(2,1)S(1)}, u32[]{:S(2)}, u32[]{:S(2)}) collective-permute-start(bf16[32,2,4,128]{3,0,2,1:T(8,128)(2,1)S(1)} %fusion.83), channel_id=1, source_target_pairs={{16,0},{32,16},{48,32},{64,48},{80,64},{96,80},{112,96},{128,112},... | collective-permute-start | bytes 196616 | tf_op jit(solution)/shard_map/ppermute | solution.py:16
  135.1 9.2 %collective-permute-start = (bf16[8,2,4,128]{3,2,1,0:T(4,128)(2,1)S(1)}, bf16[8,2,4,128]{3,2,1,0:T(4,128)(2,1)S(1)}, u32[]{:S(2)}, u32[]{:S(2)}) collective-permute-start(bf16[8,2,4,128]{3,2,1,0:T(4,128)(2,1)S(1)} %get-tuple-element.19), channel_id=1, source_target_pairs={{0,1},{1,2},{2,3},{3,4},{4,5},{5,6},{6,7},{7,8},{8,9},{9,10},{10,1... | collective-permute-start | bytes 49160 | tf_op jit(solution)/shard_map/ppermute | solution.py:14
  137.7 6.5 %collective-permute-start.1 = (bf16[8,2,4,128]{3,2,1,0:T(4,128)(2,1)S(1)}, bf16[8,2,4,128]{3,2,1,0:T(4,128)(2,1)S(1)}, u32[]{:S(2)}, u32[]{:S(2)}) collective-permute-start(bf16[8,2,4,128]{3,2,1,0:T(4,128)(2,1)S(1)} %get-tuple-element.20), channel_id=1, source_target_pairs={{1,0},{2,1},{3,2},{4,3},{5,4},{6,5},{7,6},{8,7},{9,8},{10,9},{11,1... | collective-permute-start | bytes 49160 | tf_op jit(solution)/shard_map/ppermute | solution.py:16
  155.7 59.4 %copy-start.1 = (bf16[16,2,128,128]{3,2,1,0:T(8,128)(2,1)S(1)}, bf16[16,2,128,128]{3,2,1,0:T(8,128)(2,1)}, u32[]{:S(2)}) copy-start(bf16[16,2,128,128]{3,2,1,0:T(8,128)(2,1)} %param.16) | copy-start | bytes 3145732
Sparse Core Ops, SparseCore 0:
  144.0 69.0 all-gather.1
where the time goes:
time: 225 us; the launch traced here: 224 us
  blocking collectives  115 us (51%)
  waiting for transfers between devices  53.9 us (24%)
  matrix products  26.8 us (12%)
  between operations  13.7 us (6%)
  starting transfers between devices  8.09 us (4%)
  local copies, waits for them, and re-layouts  4.17 us (2%)
    unnamed x1, blocking collectives  115 us
    all_gather x1, waiting for transfers between devices, on_device(): lax.all_gather(incoming, 'samp', axis=3, tiled=True)  53.9 us
    dot_general x4, matrix products, apply(): return jnp.einsum('bkpq,bkrq->brp', a, b, preferred_element_type=f32)  13.8 us
    dot_general x4, matrix products, radiate(): return jnp.einsum('bqu,bru->brq', a, b, preferred_element_type=f32)  5.78 us
    ppermute x2, starting transfers between devices, with_halo(): lax.ppermute(head, axis, [((i + 1) % count, i) for i in range(count)])  5.47 us
  transfers between devices with their start and end apart: 5, of which 1 were waited for; matrix products, arithmetic and copies ran while one was open for 8% of the time, Pallas kernels for 0%

commit v1 on v0

--- a/solution.py
+++ b/solution.py
@@ -118,7 +118,9 @@
     chosen = jnp.einsum(
         "ei,ihfz->ehfz",
         owner,
-        lax.all_gather(incoming, "samp", axis=3, tiled=True),
+        jnp.concatenate(
+            lax.all_to_all(jnp.stack([incoming] * lax.axis_size("samp")), "samp", 0, 0), axis=3
+        ),
         preferred_element_type=f32,
     )
     shift = phase_rows(octant)

time: 225 us -> 174 us (0.77)
  waiting for transfers between devices: 53.9 us -> 13.3 us
  between operations: 13.7 us -> 0.3 us
  starting transfers between devices: 8.09 us -> 11.9 us
    all_gather x1 -> x0, waiting for transfers between devices: 53.9 us -> none  [on_device(): lax.all_gather(incoming, 'samp', axis=3, tiled=True)]
    all_to_all x0 -> x1, waiting for transfers between devices: none -> 13.3 us  [on_device(): lax.all_to_all(jnp.stack([incoming] * lax.axis_size('samp')), 'samp', 0, 0)]
    all_to_all x0 -> x1, starting transfers between devices: none -> 3.83 us  [on_device(): lax.all_to_all(jnp.stack([incoming] * lax.axis_size('samp')), 'samp', 0, 0)]
  transfers between devices with their start and end apart: 5 -> 5, of which waited for: 1 -> 1; matrix products, arithmetic and copies ran while one was open for 8% -> 11% of each run, Pallas kernels for 0% -> 0%
where the time goes in v1:
time: 174 us; the launch traced here: 172 us
  blocking collectives  114 us (66%)
  matrix products  25.5 us (15%)
  waiting for transfers between devices  13.3 us (8%)
  starting transfers between devices  11.9 us (7%)
  local copies, waits for them, and re-layouts  5.39 us (3%)
    unnamed x1, blocking collectives  114 us
    dot_general x4, matrix products, apply(): return jnp.einsum('bkpq,bkrq->brp', a, b, preferred_element_type=f32)  13.7 us
    all_to_all x1, waiting for transfers between devices, on_device(): lax.all_to_all(jnp.stack([incoming] * lax.axis_size('samp')), 'samp', 0, 0)  13.3 us
    ppermute x2, starting transfers between devices, with_halo(): lax.ppermute(head, axis, [((i + 1) % count, i) for i in range(count)])  6.46 us
    dot_general x4, matrix products, radiate(): return jnp.einsum('bqu,bru->brq', a, b, preferred_element_type=f32)  5.79 us
    all_to_all x1, starting transfers between devices, on_device(): lax.all_to_all(jnp.stack([incoming] * lax.axis_size('samp')), 'samp', 0, 0)  3.83 us
  transfers between devices with their start and end apart: 5, of which 1 were waited for; matrix products, arithmetic and copies ran while one was open for 11% of the time, Pallas kernels for 0%

profile of v1, /device:TPU:8, one launch (start us, length us, event | category | flops | bytes accessed | tf_op | source)
XLA Modules:
  0.0 172.1 jit_solution(14544874465984397714)
XLA Ops:
  0.0 1.5 fusion.56
  1.5 1.4 fusion.58
  2.9 1.3 fusion.82
  4.2 1.4 fusion.36
  5.6 1.4 fusion.37
  7.6 0.7 convolution_bitcast_fusion
  8.4 0.7 convolution_bitcast_fusion.1
  9.3 114.1 %all-reduce.2 = bf16[16,32,2,4,128]{4,1,0,3,2:T(8,128)(2,1)} all-reduce(f32[16,32,2,4,128]{4,1,0,3,2:T(8,128)S(1)} %maximum_bitcast_fusion), channel_id=2, replica_groups=mesh['box'=16,'samp'=16] {'samp'}, use_global_device_ids=true, to_apply=%region_0.1.clone | all-reduce | flops 524288 | bytes 3145728
  123.4 0.6 dynamic-slice
  124.0 1.5 fusion.86
  125.5 1.7 %collective-permute-start.3 = (bf16[32,2,4,128]{3,0,2,1:T(8,128)(2,1)S(1)}, bf16[32,2,4,128]{3,0,2,1:T(8,128)(2,1)S(1)}, u32[]{:S(2)}, u32[]{:S(2)}) collective-permute-start(bf16[32,2,4,128]{3,0,2,1:T(8,128)(2,1)S(1)} %fusion.86), channel_id=1, source_target_pairs={{16,0},{32,16},{48,32},{64,48},{80,64},{96,80},{112,96},{128,112},... | collective-permute-start | bytes 196616 | tf_op jit(solution)/shard_map/ppermute | solution.py:16
  127.2 1.6 collective-permute-start
  128.9 4.7 %collective-permute-start.1 = (bf16[8,2,4,128]{3,2,1,0:T(4,128)(2,1)S(1)}, bf16[8,2,4,128]{3,2,1,0:T(4,128)(2,1)S(1)}, u32[]{:S(2)}, u32[]{:S(2)}) collective-permute-start(bf16[8,2,4,128]{3,2,1,0:T(4,128)(2,1)S(1)} %get-tuple-element.20), channel_id=1, source_target_pairs={{1,0},{2,1},{3,2},{4,3},{5,4},{6,5},{7,6},{8,7},{9,8},{10,9},{11,1... | collective-permute-start | bytes 49160 | tf_op jit(solution)/shard_map/ppermute | solution.py:16
  134.3 0.5 fusion.75
  134.7 0.7 subtract_reduce_fusion
  135.5 1.2 stack.67
  136.7 3.8 %all-to-all-start = ((bf16[16,32,2,4,128]{4,1,3,2,0:T(8,128)(2,1)}), bf16[16,32,2,4,128]{4,1,3,2,0:T(8,128)(2,1)S(1)}, u32[]{:S(2)}, u32[]{:S(2)}) async-start(bf16[16,32,2,4,128]{4,1,3,2,0:T(8,128)(2,1)} %stack.67), calls=%async_computation | async-start | bytes 2097152 | tf_op jit(solution)/shard_map/all_to_all | solution.py:122
  140.9 0.8 gather_fusion
  142.1 3.4 %fusion.12 = f32[16,4,128]{2,1,0:T(4,128)S(1)} fusion(bf16[16,8,2,128,128]{4,3,2,1,0:T(8,128)(2,1)} %param.13, bf16[16,8,2,4,128]{4,3,1,0,2:T(4,128)(2,1)S(1)} %broadcast_select_fusion), kind=kOutput, calls=%fused_computation.17 | convolution fusion | flops 16777216 | bytes 4358144 | tf_op jit(solution)/shard_map/bkpq,bkrq->brp/dot_general | solution.py:61
  145.5 3.4 %fusion.15 = f32[16,4,128]{2,1,0:T(4,128)S(1)} fusion(bf16[16,8,2,128,128]{4,3,2,1,0:T(8,128)(2,1)} %param.13, bf16[16,8,2,4,128]{4,3,1,0,2:T(4,128)(2,1)S(1)} %broadcast_select_fusion), kind=kOutput, calls=%fused_computation.18 | convolution fusion | flops 16777216 | bytes 4358144 | tf_op jit(solution)/shard_map/bkpq,bkrq->brp/dot_general | solution.py:61
  148.9 3.4 %fusion.31 = f32[16,4,128]{2,1,0:T(4,128)S(1)} fusion(f32[16,4,128]{2,1,0:T(4,128)S(1)} %fusion.12, bf16[16,8,2,128,128]{4,3,2,1,0:T(8,128)(2,1)} %param.13, bf16[16,8,2,4,128]{4,3,1,0,2:T(4,128)(2,1)S(1)} %broadcast_select_fusion), kind=kOutput, calls=%fused_computation.30 | convolution fusion | flops 16785408 | bytes 4390912 | tf_op jit(solution)/shard_map/bkpq,bkrq->brp/dot_general | solution.py:61
  152.3 3.5 %fusion.28 = f32[16,4,128]{2,1,0:T(4,128)S(1)} fusion(f32[16,4,128]{2,1,0:T(4,128)S(1)} %fusion.15, bf16[16,8,2,128,128]{4,3,2,1,0:T(8,128)(2,1)} %param.13, bf16[16,8,2,4,128]{4,3,1,0,2:T(4,128)(2,1)S(1)} %broadcast_select_fusion), kind=kOutput, calls=%fused_computation.29 | convolution fusion | flops 16785408 | bytes 4390912 | tf_op jit(solution)/shard_map/bkpq,bkrq->brp/dot_general | solution.py:61
  155.8 13.3 %all-to-all-done = bf16[16,32,2,4,128]{4,1,3,2,0:T(8,128)(2,1)S(1)} async-done(((bf16[16,32,2,4,128]{4,1,3,2,0:T(8,128)(2,1)}), bf16[16,32,2,4,128]{4,1,3,2,0:T(8,128)(2,1)S(1)}, u32[]{:S(2)}, u32[]{:S(2)}) %all-to-all-start) | async-done | bytes 1048608 | tf_op jit(solution)/shard_map/all_to_all | solution.py:122
  171.5 0.6 copy.87
  (54 shorter events, 4.5 us)
Async XLA Ops:
  0.0 7.1 %copy-start = (bf16[2048,128]{1,0:T(8,128)(2,1)S(1)}, bf16[2048,128]{1,0:T(8,128)(2,1)}, u32[]{:S(2)}) copy-start(bf16[2048,128]{1,0:T(8,128)(2,1)} %param.17) | copy-start | bytes 1572868
  0.0 7.5 %copy-start.7 = (s32[16]{0:T(128)S(1)}, s32[16]{0:T(128)}, u32[]{:S(2)}) copy-start(s32[16]{0:T(128)} %param.20) | copy-start | bytes 196
  8.3 115.1 %copy-start.8 = (u32[256]{0:T(256)S(1)}, u32[256]{0:T(256)}, u32[]{:S(2)}) copy-start(u32[256]{0:T(256)} %constant.68) | copy-start | bytes 3076
  8.3 118.9 %copy-start.2 = (bf16[16,2,4,128]{3,2,1,0:T(4,128)(2,1)S(1)}, bf16[16,2,4,128]{3,2,1,0:T(4,128)(2,1)}, u32[]{:S(2)}) copy-start(bf16[16,2,4,128]{3,2,1,0:T(4,128)(2,1)} %param.12) | copy-start | bytes 98308
  8.3 125.2 %copy-start.4 = (s32[32,16]{0,1:T(8,128)S(1)}, s32[32,16]{0,1:T(8,128)}, u32[]{:S(2)}) copy-start(s32[32,16]{0,1:T(8,128)} %param.23) | copy-start | bytes 6148
  8.4 125.3 %copy-start.3 = (f32[64,2,128]{2,1,0:T(2,128)S(1)}, f32[64,2,128]{2,1,0:T(2,128)}, u32[]{:S(2)}) copy-start(f32[64,2,128]{2,1,0:T(2,128)} %param.21) | copy-start | bytes 196612
  9.1 125.1 %copy-start.5 = (s32[32,16]{0,1:T(8,128)S(1)}, s32[32,16]{0,1:T(8,128)}, u32[]{:S(2)}) copy-start(s32[32,16]{0,1:T(8,128)} %param.22) | copy-start | bytes 6148
  125.5 8.8 %collective-permute-start.2 = (bf16[32,2,4,128]{3,0,2,1:T(8,128)(2,1)S(1)}, bf16[32,2,4,128]{3,0,2,1:T(8,128)(2,1)S(1)}, u32[]{:S(2)}, u32[]{:S(2)}) collective-permute-start(bf16[32,2,4,128]{3,0,2,1:T(8,128)(2,1)S(1)} %fusion.86), channel_id=1, source_target_pairs={{0,16},{16,32},{32,48},{48,64},{64,80},{80,96},{96,112},{112,128},... | collective-permute-start | bytes 196616 | tf_op jit(solution)/shard_map/ppermute | solution.py:14
  125.5 8.8 %collective-permute-start.3 = (bf16[32,2,4,128]{3,0,2,1:T(8,128)(2,1)S(1)}, bf16[32,2,4,128]{3,0,2,1:T(8,128)(2,1)S(1)}, u32[]{:S(2)}, u32[]{:S(2)}) collective-permute-start(bf16[32,2,4,128]{3,0,2,1:T(8,128)(2,1)S(1)} %fusion.86), channel_id=1, source_target_pairs={{16,0},{32,16},{48,32},{64,48},{80,64},{96,80},{112,96},{128,112},... | collective-permute-start | bytes 196616 | tf_op jit(solution)/shard_map/ppermute | solution.py:16
  127.2 13.6 %collective-permute-start = (bf16[8,2,4,128]{3,2,1,0:T(4,128)(2,1)S(1)}, bf16[8,2,4,128]{3,2,1,0:T(4,128)(2,1)S(1)}, u32[]{:S(2)}, u32[]{:S(2)}) collective-permute-start(bf16[8,2,4,128]{3,2,1,0:T(4,128)(2,1)S(1)} %get-tuple-element.19), channel_id=1, source_target_pairs={{0,1},{1,2},{2,3},{3,4},{4,5},{5,6},{6,7},{7,8},{8,9},{9,10},{10,1... | collective-permute-start | bytes 49160 | tf_op jit(solution)/shard_map/ppermute | solution.py:14
  128.9 12.0 %collective-permute-start.1 = (bf16[8,2,4,128]{3,2,1,0:T(4,128)(2,1)S(1)}, bf16[8,2,4,128]{3,2,1,0:T(4,128)(2,1)S(1)}, u32[]{:S(2)}, u32[]{:S(2)}) collective-permute-start(bf16[8,2,4,128]{3,2,1,0:T(4,128)(2,1)S(1)} %get-tuple-element.20), channel_id=1, source_target_pairs={{1,0},{2,1},{3,2},{4,3},{5,4},{6,5},{7,6},{8,7},{9,8},{10,9},{11,1... | collective-permute-start | bytes 49160 | tf_op jit(solution)/shard_map/ppermute | solution.py:16
  134.2 6.3 %copy-start.6 = (s32[16,8]{0,1:T(8,128)S(1)}, s32[16,8]{0,1:T(8,128)}, u32[]{:S(2)}) copy-start(s32[16,8]{0,1:T(8,128)} %param.14) | copy-start | bytes 1540
  136.7 32.4 %all-to-all-start = ((bf16[16,32,2,4,128]{4,1,3,2,0:T(8,128)(2,1)}), bf16[16,32,2,4,128]{4,1,3,2,0:T(8,128)(2,1)S(1)}, u32[]{:S(2)}, u32[]{:S(2)}) async-start(bf16[16,32,2,4,128]{4,1,3,2,0:T(8,128)(2,1)} %stack.67), calls=%async_computation | async-start | bytes 2097152 | tf_op jit(solution)/shard_map/all_to_all | solution.py:122
  152.3 17.6 %copy-start.1 = (bf16[16,2,128,128]{3,2,1,0:T(8,128)(2,1)S(1)}, bf16[16,2,128,128]{3,2,1,0:T(8,128)(2,1)}, u32[]{:S(2)}) copy-start(bf16[16,2,128,128]{3,2,1,0:T(8,128)(2,1)} %param.16) | copy-start | bytes 3145732
